TPU v7x, 32 devices: a whole 2x2x4 slice. The times are simulated.
32 devices in a mesh: dp: 8 (over y, x, core), fsdp: 4 (over z).
Axes of the slice: x: 2, y: 2, z: 4, core: 2. Of those that a mesh axis runs over, the one named last changes fastest.
Arguments:
- inputs: bfloat16 [32, 8, 12, 6, 6, 256], P(('dp', 'fsdp')), may hold values from -6 to 6
- cotangent: bfloat16 [32, 8, 12, 6, 6, 256], P(('dp', 'fsdp')), may hold values from -6 to 6
- lengths: int32 [32], P(('dp', 'fsdp')), may hold values from 2 to 8
- face_table: int32 [12, 4], replicated, may hold values from 0 to 11
- w_first: float32 [2304, 256], P('fsdp'), may hold values from -0.125 to 0.125
- w_second: float32 [2304, 256], P('fsdp'), may hold values from -0.125 to 0.125
- w_skip: float32 [256, 256], P('fsdp'), may hold values from -0.375 to 0.375
- mom_first: float32 [2304, 256], P('fsdp'), may hold values from -64 to 64
- sq_first: float32 [2304, 256], P('fsdp'), may hold values from 12.16512 to 48.66048
- mom_second: float32 [2304, 256], P('fsdp'), may hold values from -64 to 64
- sq_second: float32 [2304, 256], P('fsdp'), may hold values from 12.16512 to 48.66048
- mom_skip: float32 [256, 256], P('fsdp'), may hold values from -160 to 160
- sq_skip: float32 [256, 256], P('fsdp'), may hold values from 68.56704 to 276.48
Outputs:
- output: bfloat16 [32, 8, 12, 6, 6, 256], P(('dp', 'fsdp'))
- grad_inputs: float32 [32, 8, 12, 6, 6, 256], P(('dp', 'fsdp'))
- new_first: float32 [2304, 256], P('fsdp')
- new_mom_first: float32 [2304, 256], P('fsdp')
- new_sq_first: float32 [2304, 256], P('fsdp')
- new_second: float32 [2304, 256], P('fsdp')
- new_mom_second: float32 [2304, 256], P('fsdp')
- new_sq_second: float32 [2304, 256], P('fsdp')
- new_skip: float32 [256, 256], P('fsdp')
- new_mom_skip: float32 [256, 256], P('fsdp')
- new_sq_skip: float32 [256, 256], P('fsdp')
All inputs are finite; a program needn't handle non-finite values.
Results may differ from a plain program's by a relative error of at most 0.019.
Values may be sent and summed in bfloat16 or wider, within the bound.
No kernel may reach another device: no remote copies, remote signals or barrier semaphores. Data moves between devices by JAX's collectives and lax.ppermute only.
A program may use at most 256 MiB of HBM per device.

v0:
```python
import jax
import jax.numpy as jnp
from jax import lax
from jax.sharding import PartitionSpec as P

C = 256
STEP_COUNT = 10
tap_offsets = [(row_off, col_off) for row_off in range(3) for col_off in range(3)]


def face_hots(face_table, dtype):
    faces = face_table.shape[0]
    labels = jnp.arange(faces, dtype=jnp.int32)
    return [
        (face_table[:, corner_side][:, None] == labels[None, :]).astype(dtype)
        for corner_side in range(4)
    ]


def pad_faces(field, hots):

    def route(matrix, edge, form):
        return jnp.einsum(form, matrix, edge, preferred_element_type=jnp.float32).astype(
            jnp.bfloat16
        )

    north = route(hots[0], field[:, :, -1], "fh,rhwc->rfwc")
    east = route(hots[1], field[:, :, :, 0], "fh,rhwc->rfwc")
    south = route(hots[2], field[:, :, 0], "fh,rhwc->rfwc")
    west = route(hots[3], field[:, :, :, -1], "fh,rhwc->rfwc")
    middle = jnp.concatenate([west[:, :, :, None], field, east[:, :, :, None]], axis=3)
    top_row = jnp.pad(north, ((0, 0), (0, 0), (1, 1), (0, 0)))
    bottom_row = jnp.pad(south, ((0, 0), (0, 0), (1, 1), (0, 0)))
    return jnp.concatenate([top_row[:, :, None], middle, bottom_row[:, :, None]], axis=2)


def unpad_back(spread, hots):
    highest = lax.Precision.HIGHEST
    inner = spread[:, :, 1:-1, 1:-1]
    inner = inner.at[:, :, -1].add(
        jnp.einsum("fh,rfwc->rhwc", hots[0], spread[:, :, 0, 1:-1], precision=highest)
    )
    inner = inner.at[:, :, :, 0].add(
        jnp.einsum("fh,rfwc->rhwc", hots[1], spread[:, :, 1:-1, -1], precision=highest)
    )
    inner = inner.at[:, :, 0].add(
        jnp.einsum("fh,rfwc->rhwc", hots[2], spread[:, :, -1, 1:-1], precision=highest)
    )
    inner = inner.at[:, :, :, -1].add(
        jnp.einsum("fh,rfwc->rhwc", hots[3], spread[:, :, 1:-1, 0], precision=highest)
    )
    return inner


def conv_apply(padded, weight):
    edge_len = padded.shape[2] - 2
    channels = weight.shape[1]
    taps_weight = weight.reshape(9, channels, channels)
    flat_padded = padded.reshape(-1, channels)
    products = jnp.einsum(
        "pc,tcd->ptd", flat_padded, taps_weight, preferred_element_type=jnp.float32
    )
    products = products.reshape(padded.shape[:4] + (9, channels))
    summed = None
    for tap_index, (row_off, col_off) in enumerate(tap_offsets):
        part = products[:, :, row_off : row_off + edge_len, col_off : col_off + edge_len, tap_index]
        summed = part if summed is None else summed + part
    return summed


def conv_back(padded, grad, weight):
    channels = weight.shape[1]
    taps_weight = weight.reshape(9, channels, channels)
    flat_grad = grad.reshape(-1, channels)
    pulled = jnp.einsum("pd,tcd->ptc", flat_grad, taps_weight, preferred_element_type=jnp.float32)
    pulled = pulled.reshape(grad.shape[:4] + (9, channels))
    spread = None
    placed = []
    for tap_index, (row_off, col_off) in enumerate(tap_offsets):
        widths = ((0, 0), (0, 0), (row_off, 2 - row_off), (col_off, 2 - col_off), (0, 0))
        moved = jnp.pad(pulled[:, :, :, :, tap_index], widths)
        spread = moved if spread is None else spread + moved
        placed.append(jnp.pad(grad, widths))
    stacked = jnp.stack(placed, axis=4).reshape(-1, 9, channels)
    flat_padded = padded.reshape(-1, channels)
    weight_grad = jnp.einsum(
        "pc,ptd->tcd", flat_padded, stacked, preferred_element_type=jnp.float32
    )
    return (weight_grad.reshape(9 * channels, channels), spread)


def gelu_tanh(v):
    return jax.nn.gelu(v, approximate=True)


def forward_pass(fields, hots_low, gathered):
    pad_in = pad_faces(fields, hots_low)
    pre_one = conv_apply(pad_in, gathered[0])
    hidden = gelu_tanh(pre_one).astype(jnp.bfloat16)
    pad_hidden = pad_faces(hidden, hots_low)
    pre_two = conv_apply(pad_hidden, gathered[1])
    return (pad_in, pre_one, pad_hidden, pre_two)


def adamw(weight, moment, square, grad, rate):
    moment_new = 0.9 * moment + 0.1 * grad
    square_new = 0.999 * square + 0.001 * grad * grad
    fix_one = 1.0 - 0.9**STEP_COUNT
    fix_two = 1.0 - 0.999**STEP_COUNT
    weight_new = weight - rate * (
        moment_new / fix_one / (jnp.sqrt(square_new / fix_two) + 1e-08) + 0.01 * weight
    )
    return (weight_new, moment_new, square_new)


def per_device(
    inputs,
    cotangent,
    lengths,
    face_table,
    w_first,
    w_second,
    w_skip,
    mom_first,
    sq_first,
    mom_second,
    sq_second,
    mom_skip,
    sq_skip,
):
    fields = inputs[0]
    channels = fields.shape[-1]
    hots_low = face_hots(face_table, jnp.bfloat16)
    hots_full = face_hots(face_table, jnp.float32)
    low_weights = (
        w_first.astype(jnp.bfloat16),
        w_second.astype(jnp.bfloat16),
        w_skip.astype(jnp.bfloat16),
    )
    gathered = (
        lax.all_gather(low_weights[0], "fsdp", axis=0, tiled=True),
        lax.all_gather(low_weights[1], "fsdp", axis=0, tiled=True),
        lax.all_gather(low_weights[2], "fsdp", axis=0, tiled=True),
    )
    saved = forward_pass(fields, hots_low, gathered)
    flat_fields = fields.reshape(-1, channels)
    skipped = jnp.dot(flat_fields, gathered[2], preferred_element_type=jnp.float32).reshape(
        fields.shape
    )
    output = (gelu_tanh(saved[3]) + skipped).astype(jnp.bfloat16)
    gathered = (
        lax.all_gather(low_weights[0], "fsdp", axis=0, tiled=True),
        lax.all_gather(low_weights[1], "fsdp", axis=0, tiled=True),
        lax.all_gather(low_weights[2], "fsdp", axis=0, tiled=True),
    )
    saved = forward_pass(fields, hots_low, gathered)
    pad_in, pre_one, pad_hidden, pre_two = saved
    live = (jnp.arange(fields.shape[0]) < lengths[0]).astype(jnp.bfloat16)
    grad_out = cotangent[0] * live[:, None, None, None, None]
    flat_out = grad_out.reshape(-1, channels)
    dw_skip = lax.dot_general(
        flat_fields, flat_out, (((0,), (0,)), ((), ())), preferred_element_type=jnp.float32
    )
    gelu_pull_two = jax.vjp(gelu_tanh, pre_two)[1]
    grad_two = gelu_pull_two(grad_out.astype(jnp.float32))[0].astype(jnp.bfloat16)
    dw_second, spread_hidden = conv_back(pad_hidden, grad_two, gathered[1])
    grad_hidden = unpad_back(spread_hidden, hots_full)
    gelu_pull_one = jax.vjp(gelu_tanh, pre_one)[1]
    grad_one = gelu_pull_one(grad_hidden)[0].astype(jnp.bfloat16)
    dw_first, spread_in = conv_back(pad_in, grad_one, gathered[0])
    skip_back = lax.dot_general(
        flat_out, gathered[2], (((1,), (1,)), ((), ())), preferred_element_type=jnp.float32
    )
    grad_inputs = unpad_back(spread_in, hots_full) + skip_back.reshape(fields.shape)
    shards = (
        lax.psum_scatter(
            dw_first.astype(jnp.bfloat16), "fsdp", scatter_dimension=0, tiled=True
        ).astype(jnp.float32),
        lax.psum_scatter(
            dw_second.astype(jnp.bfloat16), "fsdp", scatter_dimension=0, tiled=True
        ).astype(jnp.float32),
        lax.psum_scatter(
            dw_skip.astype(jnp.bfloat16), "fsdp", scatter_dimension=0, tiled=True
        ).astype(jnp.float32),
    )
    rate_conv = (9 * C) ** (-0.5)
    rate_skip = C ** (-0.5)
    totals = (
        lax.psum(shards[0].astype(jnp.bfloat16), "dp").astype(jnp.float32),
        lax.psum(shards[1].astype(jnp.bfloat16), "dp").astype(jnp.float32),
        lax.psum(shards[2].astype(jnp.bfloat16), "dp").astype(jnp.float32),
    )
    first_set = adamw(w_first, mom_first, sq_first, totals[0], rate_conv)
    second_set = adamw(w_second, mom_second, sq_second, totals[1], rate_conv)
    skip_set = adamw(w_skip, mom_skip, sq_skip, totals[2], rate_skip)
    return (
        output[None],
        grad_inputs[None],
        first_set[0],
        first_set[1],
        first_set[2],
        second_set[0],
        second_set[1],
        second_set[2],
        skip_set[0],
        skip_set[1],
        skip_set[2],
    )


def solution(mesh):
    placed = (
        P(("dp", "fsdp"), None, None, None, None, None),
        P(("dp", "fsdp"), None, None, None, None, None),
        P(("dp", "fsdp")),
        P(),
        P("fsdp", None),
        P("fsdp", None),
        P("fsdp", None),
        P("fsdp", None),
        P("fsdp", None),
        P("fsdp", None),
        P("fsdp", None),
        P("fsdp", None),
        P("fsdp", None),
    )
    return jax.shard_map(
        per_device,
        mesh=mesh,
        in_specs=placed,
        out_specs=(
            P(("dp", "fsdp"), None, None, None, None, None),
            P(("dp", "fsdp"), None, None, None, None, None),
            P("fsdp", None),
            P("fsdp", None),
            P("fsdp", None),
            P("fsdp", None),
            P("fsdp", None),
            P("fsdp", None),
            P("fsdp", None),
            P("fsdp", None),
            P("fsdp", None),
        ),
        check_vma=False,
    )
```

profile of v0, /device:TPU:0, one launch (start us, length us, event | category | flops | bytes accessed | tf_op | source)
XLA Modules:
  0.0 511.8 jit_solution(13693216425621798046)
XLA Ops:
  7.9 5.0 fusion.84
  12.9 0.8 copy.411
  15.4 2.5 copy.510
  18.0 2.2 fusion.39
  22.2 2.4 maximum_bitcast_fusion
  24.7 11.0 %reduce-scatter.10.cloned.1.call-done = bf16[64,256]{1,0:T(8,128)(2,1)} async-done(((bf16[256,256]{1,0:T(8,128)(2,1)}), bf16[64,256]{1,0:T(8,128)(2,1)}) %reduce-scatter.10.cloned.1.call-update) | async-done | bytes 32784 | tf_op jit(solution)/shard_map/reduce_scatter | solution.py:182
  35.7 23.7 %psum.23 = bf16[64,256]{1,0:T(8,128)(2,1)S(1)} all-reduce(bf16[64,256]{1,0:T(8,128)(2,1)} %reduce-scatter.10.cloned.1.call-done), channel_id=1, replica_groups=mesh['dp'=8,'fsdp'=4] {'dp'}, use_global_device_ids=true, to_apply=%region_5.6 | all-reduce | flops 16384 | bytes 65536 | tf_op jit(solution)/shard_map/psum | solution.py:191
  60.2 14.7 %all_gather.14 = bf16[256,256]{1,0:T(8,128)(2,1)} all-gather(bf16[64,256]{1,0:T(8,128)(2,1)S(1)} %get-tuple-element.194), channel_id=1, replica_groups=mesh['dp'=8,'fsdp'=4] {'fsdp'}, dimensions={0}, use_global_device_ids=true | all-gather | bytes 163840 | tf_op jit(solution)/shard_map/all_gather | solution.py:143
  74.8 24.0 %fusion.33 = f32[8,12,8,8,9,256]{5,3,4,2,1,0:T(8,128)} fusion(bf16[9,256,256,1,1,1]{2,1,0,5,4,3:T(8,128)(2,1)} %bitcast.404, bf16[8,12,8,8,256,1]{4,1,3,0,2,5:T(8,128)(2,1)} %maximum_bitcast_fusion), kind=kOutput, calls=%fused_computation.102 | convolution fusion | flops 7247757312 | bytes 60948480 | tf_op jit(solution)/shard_map/pc,tcd->ptd/dot_general | solution.py:60
  98.8 17.8 %multiply_convert_fusion = (bf16[8,12,6,6,256]{4,3,2,1,0:T(8,128)(2,1)S(1)}, f32[8,12,6,6,256]{4,3,2,1,0:T(8,128)}) fusion(f32[8,12,8,8,9,256]{5,3,4,2,1,0:T(8,128)} %fusion.33), kind=kLoop, calls=%fused_computation.78 | loop fusion | flops 15040512 | bytes 37158912 | tf_op jit(solution)/shard_map/convert_element_type | solution.py:99
  117.2 1.1 copy.300
  118.8 1.0 copy.301
  119.8 0.8 fusion.176
  122.3 0.8 copy-done.15
  123.0 22.2 %fusion.115 = f32[8,12,8,8,9,256]{5,3,2,1,0,4:T(8,128)} fusion(bf16[9,256,256,1,1,1]{2,1,5,4,3,0:T(8,128)(2,1)} %bitcast.402, bf16[8,12,1,8,256]{4,3,2,1,0:T(8,128)(2,1)} %copy.301, bf16[8,12,6,1,256]{4,3,2,1,0:T(2,128)(2,1)S(1)} %copy.296, bf16[8,12,6,6,256]{4,3,2,1,0:T(8,128)(2,1)S(1)} %get-tuple-element.164, bf16[8,12,6,1,256]{4,3,2,1,0:T(2,128)(2,1)S(1)} %copy.295, ...), kind=kOutput, calls=%fused_computation.210 | convolution fusion | flops 7263485952 | bytes 60948480 | tf_op jit(solution)/shard_map/pc,tcd->ptd/dot_general | solution.py:60
  145.3 18.2 %fusion.7 = (bf16[8,12,6,6,256]{4,3,2,1,0:T(8,128)(2,1)S(1)}, f32[8,12,6,6,1,256]{5,3,2,1,0,4:T(8,128)}) fusion(bf16[8]{0:T(256)(128)(2,1)S(1)} %copy-done.29, bf16[1,8,12,6,6,256]{5,1,4,3,2,0:T(8,128)(2,1)S(1)} %copy-done.1, f32[8,12,8,8,9,256]{5,3,2,1,0,4:T(8,128)} %fusion.115), kind=kLoop, calls=%fused_computation.19 | loop fusion | flops 26542080 | bytes 38928400 | tf_op jit(solution)/shard_map/convert_element_type | solution.py:165
  163.5 19.7 %fusion.40 = f32[8,12,6,6,9,256]{5,3,2,1,0,4:T(8,128)} fusion(bf16[9,256,256,1,1,1]{2,1,5,4,3,0:T(8,128)(2,1)S(1)} %bitcast.403, f32[8,12,6,6,1,256]{5,3,2,1,0,4:T(8,128)} %get-tuple-element.163, bf16[1,8,12,6,6,256]{5,1,4,3,2,0:T(8,128)(2,1)} %param.30, bf16[8]{0:T(256)(128)(2,1)} %copy-done.28), kind=kOutput, calls=%fused_computation.113 | convolution fusion | flops 4098097152 | bytes 38338576 | tf_op jit(solution)/shard_map/pd,tcd->ptc/dot_general | solution.py:75
  183.2 30.6 %slice_bitcast_fusion.17 = (f32[8,12,6,6,256]{4,3,2,1,0:T(8,128)}, f32[8,12,6,6,256]{4,3,2,1,0:T(8,128)}, f32[8,12,6,6,256]{4,3,2,1,0:T(8,128)}, f32[8,12,6,6,25...) fusion(f32[8,12,6,6,9,256]{5,3,2,1,0,4:T(8,128)} %fusion.40), kind=kLoop, calls=%fused_computation.56 | loop fusion | bytes 63700992 | tf_op jit(solution)/shard_map/squeeze | solution.py:81
  213.8 18.5 %pad_add_fusion.1 = f32[8,12,8,8,256]{4,3,2,1,0:T(8,128)} fusion(f32[8,12,6,6,256]{4,3,2,1,0:T(8,128)} %get-tuple-element.183, f32[8,12,6,6,256]{4,3,2,1,0:T(8,128)} %get-tuple-element.176, f32[8,12,6,6,256]{4,3,2,1,0:T(8,128)} %get-tuple-element.177, f32[8,12,6,6,256]{4,3,2,1,0:T(8,128)} %get-tuple-element.178, f32[8,12,6,6,256]{4,3,2,1,0:T(8,128)} %get-tuple-element.179, ...), kind=kLoop, calls=%fused_computation.7 | loop fusion | flops 12582912 | bytes 38141952 | tf_op jit(solution)/shard_map/add | solution.py:82
  232.3 4.9 fusion.175
  237.2 2.7 slice_bitcast_fusion.26
  239.9 5.3 %slice.563 = f32[8,12,6,6,256]{4,3,2,1,0:T(8,128)} slice(f32[8,12,8,8,256]{4,3,2,1,0:T(8,128)} %pad_add_fusion.1), slice={[0:8], [0:12], [1:7], [1:7], [0:256]} | slice | bytes 7077888 | tf_op jit(solution)/shard_map/slice | solution.py:39
  245.2 2.3 bitcast_dynamic-update-slice_fusion.8
  247.5 2.5 bitcast_dynamic-update-slice_fusion.7
  249.9 2.5 bitcast_dynamic-update-slice_fusion.6
  252.4 2.4 bitcast_dynamic-update-slice_fusion.5
  254.8 2.4 bitcast_dynamic-update-slice_fusion.4
  257.2 2.4 bitcast_dynamic-update-slice_fusion.3
  259.7 2.4 bitcast_dynamic-update-slice_fusion.2
  262.1 2.5 bitcast_dynamic-update-slice_fusion.1
  264.5 2.4 bitcast_dynamic-update-slice_fusion
  267.0 13.9 %bitcast_convert_fusion = bf16[9,256,256]{1,2,0:T(8,128)(2,1)} fusion(bf16[8,12,8,8,9,256]{5,3,2,1,0,4:T(8,128)(2,1)} %bitcast_dynamic-update-slice_fusion, bf16[8,12,1,8,256]{4,3,2,1,0:T(8,128)(2,1)S(1)} %copy-done.19, bf16[8,12,6,1,256]{4,3,2,1,0:T(2,128)(2,1)S(1)} %copy-done.16, bf16[8,12,6,6,256]{4,3,2,1,0:T(8,128)(2,1)S(1)} %copy-done.3, ...), kind=kOutput, calls=%fused_computation.111 | convolution fusion | flops 7264075776 | bytes 32636928 | tf_op jit(solution)/shard_map/pc,ptd->tcd/dot_general | solution.py:86
  283.8 2.6 fusion.90
  286.4 3.2 slice_add_fusion.19
  289.6 13.0 %scatter-add.29 = f32[8,12,6,6,256]{4,3,2,1,0:T(8,128)} dynamic-update-slice(f32[8,12,6,6,256]{4,3,2,1,0:T(8,128)} %fusion.90, f32[8,12,6,1,256]{4,3,2,1,0:T(1,128)S(1)} %slice_add_fusion.19, s32[]{:T(128)} %constant.226.clone.1, s32[]{:T(128)} %constant.226.clone.1, s32[]{:T(128)} %constant.226.clone.1, s32[]{:T(128)} %constant.226.clone.1, s32[]{:T(128)} %constant.226.clone.1) | dynamic-update-slice | bytes 1179652 | tf_op jit(solution)/shard_map/scatter-add | solution.py:43
  302.6 2.5 fusion.89
  305.1 3.4 slice_add_fusion.18
  308.5 13.0 %scatter-add.31 = f32[8,12,6,6,256]{4,3,2,1,0:T(8,128)} dynamic-update-slice(f32[8,12,6,6,256]{4,3,2,1,0:T(8,128)} %fusion.89, f32[8,12,6,1,256]{4,3,2,1,0:T(1,128)S(1)} %slice_add_fusion.18, s32[]{:T(128)} %constant.226.clone.1, s32[]{:T(128)} %constant.226.clone.1, s32[]{:T(128)} %constant.226.clone.1, s32[]{:T(128)} %constant.227.clone.1, s32[]{:T(128)} %constant.226.clone.1) | dynamic-update-slice | bytes 1179652 | tf_op jit(solution)/shard_map/scatter-add | solution.py:49
  321.5 5.5 %fusion.16 = bf16[8,12,6,6,256]{4,3,2,1,0:T(8,128)(2,1)S(1)} fusion(f32[8,12,6,6,256]{4,3,2,1,0:T(8,128)} %get-tuple-element.165, f32[8,12,6,6,256]{4,3,2,1,0:T(8,128)} %scatter-add.31), kind=kLoop, calls=%fused_computation.28 | loop fusion | flops 17694720 | bytes 8847360 | tf_op jit(solution)/shard_map/convert_element_type | solution.py:169
  327.0 2.3 bitcast_dynamic-update-slice_fusion.17
  329.3 2.4 bitcast_dynamic-update-slice_fusion.16
  331.8 2.4 bitcast_dynamic-update-slice_fusion.15
  334.2 2.3 bitcast_dynamic-update-slice_fusion.14
  336.5 2.4 bitcast_dynamic-update-slice_fusion.13
  338.9 2.4 bitcast_dynamic-update-slice_fusion.12
  341.4 2.4 bitcast_dynamic-update-slice_fusion.11
  343.8 2.4 bitcast_dynamic-update-slice_fusion.10
  346.2 2.5 bitcast_dynamic-update-slice_fusion.9
  348.7 16.7 %fusion.43 = f32[8,12,6,6,9,256]{5,1,4,3,2,0:T(8,128)} fusion(bf16[9,256,256,1,1,1]{2,1,0,5,4,3:T(8,128)(2,1)S(1)} %bitcast.405, bf16[8,12,6,6,256,1]{4,3,2,1,0,5:T(8,128)(2,1)S(1)} %bitcast.397), kind=kOutput, calls=%fused_computation.116 | convolution fusion | flops 4076863488 | bytes 34799616 | tf_op jit(solution)/shard_map/pd,tcd->ptc/dot_general | solution.py:75
  365.3 31.7 %slice_bitcast_fusion.8 = (f32[8,12,6,6,256]{4,1,3,2,0:T(8,128)}, f32[8,12,6,6,256]{4,1,3,2,0:T(8,128)}, f32[8,12,6,6,256]{4,1,3,2,0:T(8,128)}, f32[8,12,6,6,256...) fusion(f32[8,12,6,6,9,256]{5,1,4,3,2,0:T(8,128)} %fusion.43), kind=kLoop, calls=%fused_computation.47 | loop fusion | bytes 63700992 | tf_op jit(solution)/shard_map/squeeze | solution.py:81
  397.0 15.3 %bitcast_convert_fusion.1 = bf16[9,256,256]{1,2,0:T(8,128)(2,1)} fusion(bf16[8,12,8,8,9,256]{5,3,2,1,0,4:T(8,128)(2,1)} %bitcast_dynamic-update-slice_fusion.9, bf16[8,12,8,8,256,1]{4,1,3,0,2,5:T(8,128)(2,1)} %maximum_bitcast_fusion), kind=kOutput, calls=%fused_computation.112 | convolution fusion | flops 7248347136 | bytes 32636928 | tf_op jit(solution)/shard_map/pc,ptd->tcd/dot_general | solution.py:86
  412.4 4.9 fusion.53
  417.3 3.1 copy.352
  420.4 14.8 %pad_add_fusion = f32[8,12,8,8,256]{4,1,3,2,0:T(8,128)S(1)} fusion(f32[8,12,6,6,256]{4,1,3,2,0:T(8,128)} %get-tuple-element.173, f32[8,12,6,6,256]{4,1,3,2,0:T(8,128)} %get-tuple-element.174, f32[8,12,6,6,256]{4,1,3,2,0:T(8,128)} %get-tuple-element.167, f32[8,12,6,6,256]{4,1,3,2,0:T(8,128)} %get-tuple-element.168, f32[8,12,6,6,256]{4,1,3,2,0:T(8,128)} %get-tuple-element.169, ...), kind=kLoop, calls=%fused_computation | loop fusion | flops 12582912 | bytes 38141952 | tf_op jit(solution)/shard_map/add | solution.py:82
  435.3 2.7 slice.581
  438.0 1.4 fusion.61
  439.4 2.6 fusion.63
  442.0 2.5 fusion.65
  444.5 2.5 fusion.67
  447.1 3.3 add_bitcast_fusion
  450.4 3.8 copy.353
  454.3 45.6 %all-reduce.43.cloned.1.call-done = (bf16[576,256]{1,0:T(8,128)(2,1)}, bf16[576,256]{1,0:T(8,128)(2,1)}) async-done(((bf16[576,256]{1,0:T(8,128)(2,1)}, bf16[576,256]{1,0:T(8,128)(2,1)}), (bf16[576,256]{1,0:T(8,128)(2,1)}, bf16[576,256]{1,0:T(8,128)(2,1)})) %all-reduce.43.cloned.1.call-update) | async-done | bytes 589840 | tf_op jit(solution)/shard_map/psum | solution.py:189
  499.8 2.4 multiply_subtract_fusion.1
  502.3 2.4 multiply_subtract_fusion
  (107 shorter events, 10.1 us)
Async XLA Ops:
  7.2 28.6 %reduce-scatter.10.cloned.1.call-start = ((), (), s32[]{:S(2)}) async-start(), calls=%async_computation.7 | async-start | bytes 163840 | tf_op jit(solution)/shard_map/reduce_scatter | solution.py:182
  7.9 10.1 %copy-start.28 = (bf16[8]{0:T(256)(128)(2,1)}, bf16[8]{0:T(256)(128)(2,1)S(1)}, u32[]{:S(2)}) copy-start(bf16[8]{0:T(256)(128)(2,1)S(1)} %compare_convert_fusion) | copy-start | bytes 52
  7.9 5.9 %copy-start.9 = (f32[576,256]{1,0:T(8,128)S(1)}, f32[576,256]{1,0:T(8,128)}, u32[]{:S(2)}) copy-start(f32[576,256]{1,0:T(8,128)} %param.33) | copy-start | bytes 1769476
  7.9 6.7 %copy-start.11 = (f32[576,256]{1,0:T(8,128)S(1)}, f32[576,256]{1,0:T(8,128)}, u32[]{:S(2)}) copy-start(f32[576,256]{1,0:T(8,128)} %param.34) | copy-start | bytes 1769476
  12.9 5.1 copy-start
  13.7 61.1 %all-gather.3.cloned.1.call-start = ((), (), s32[]{:S(2)}) async-start(), calls=%async_computation.3 | async-start | bytes 1474560 | tf_op jit(solution)/shard_map/all_gather | solution.py:141
  14.5 5.6 %copy-start.30 = (s32[12,4]{0,1:T(4,128)S(1)}, s32[12,4]{0,1:T(4,128)}, u32[]{:S(2)}) copy-start(s32[12,4]{0,1:T(4,128)} %param.32) | copy-start | bytes 580
  14.5 107.7 %all-gather.5.cloned.1.call-start = ((), (), s32[]{:S(2)}) async-start(), calls=%async_computation.4 | async-start | bytes 1474560 | tf_op jit(solution)/shard_map/all_gather | solution.py:142
  15.4 431.7 %reduce-scatter.8.cloned.1.call-start = ((), (), s32[]{:S(2)}) async-start(), calls=%async_computation.6 | async-start | bytes 1474560 | tf_op jit(solution)/shard_map/reduce_scatter | solution.py:179
  22.1 37.4 %copy-start.25 = (f32[64,256]{1,0:T(8,128)S(1)}, f32[64,256]{1,0:T(8,128)}, u32[]{:S(2)}) copy-start(f32[64,256]{1,0:T(8,128)} %param.35) | copy-start | bytes 196612
  22.1 37.4 %copy-start.26 = (f32[64,256]{1,0:T(8,128)S(1)}, f32[64,256]{1,0:T(8,128)}, u32[]{:S(2)}) copy-start(f32[64,256]{1,0:T(8,128)} %param.40) | copy-start | bytes 196612
  22.1 37.4 %copy-start.27 = (f32[64,256]{1,0:T(8,128)S(1)}, f32[64,256]{1,0:T(8,128)}, u32[]{:S(2)}) copy-start(f32[64,256]{1,0:T(8,128)} %param.41) | copy-start | bytes 196612
  116.6 5.7 %copy-start.2 = (bf16[8,12,6,6,256]{4,3,2,1,0:T(8,128)(2,1)}, bf16[8,12,6,6,256]{4,3,2,1,0:T(8,128)(2,1)S(1)}, u32[]{:S(2)}) copy-start(bf16[8,12,6,6,256]{4,3,2,1,0:T(8,128)(2,1)S(1)} %get-tuple-element.164) | copy-start | bytes 5308420
  121.4 0.9 copy-start.13
  122.2 0.8 copy-start.15
  123.0 22.3 %copy-start.1 = (bf16[1,8,12,6,6,256]{5,1,4,3,2,0:T(8,128)(2,1)S(1)}, bf16[1,8,12,6,6,256]{5,1,4,3,2,0:T(8,128)(2,1)}, u32[]{:S(2)}) copy-start(bf16[1,8,12,6,6,256]{5,1,4,3,2,0:T(8,128)(2,1)} %param.30) | copy-start | bytes 5308420
  123.0 22.3 %copy-start.29 = (bf16[8]{0:T(256)(128)(2,1)S(1)}, bf16[8]{0:T(256)(128)(2,1)}, u32[]{:S(2)}) copy-start(bf16[8]{0:T(256)(128)(2,1)} %copy-done.28) | copy-start | bytes 52
  145.3 18.2 %copy-start.5 = (bf16[2304,256]{1,0:T(8,128)(2,1)S(1)}, bf16[2304,256]{1,0:T(8,128)(2,1)}, u32[]{:S(2)}) copy-start(bf16[2304,256]{1,0:T(8,128)(2,1)} %all-gather.5.cloned.1.call-done) | copy-start | bytes 3538948
  262.0 4.9 copy-start.3
  262.0 4.9 copy-start.14
  262.0 4.9 copy-start.16
  262.0 4.9 copy-start.18
  262.0 4.9 copy-start.19
  280.9 1.5 copy-start.8
  280.9 2.2 copy-start.7
  280.9 166.2 %reduce-scatter.6.cloned.1.call-start = ((), (), s32[]{:S(2)}) async-start(), calls=%async_computation.5 | async-start | bytes 1474560 | tf_op jit(solution)/shard_map/reduce_scatter | solution.py:176
  343.8 4.9 copy-start.6
  397.0 15.4 %copy-start.17 = (bf16[1,8,12,6,6,256]{5,1,4,3,2,0:T(8,128)(2,1)S(1)}, bf16[1,8,12,6,6,256]{5,1,4,3,2,0:T(8,128)(2,1)}, u32[]{:S(2)}) copy-start(bf16[1,8,12,6,6,256]{5,1,4,3,2,0:T(8,128)(2,1)} %param.29) | copy-start | bytes 5308420
  397.0 15.4 %copy-start.24 = (bf16[256,256]{1,0:T(8,128)(2,1)S(1)}, bf16[256,256]{1,0:T(8,128)(2,1)}, u32[]{:S(2)}) copy-start(bf16[256,256]{1,0:T(8,128)(2,1)} %all_gather.14) | copy-start | bytes 393220
  412.4 87.5 %all-reduce.43.cloned.1.call-start = ((), (), s32[]{:S(2)}) async-start(), calls=%async_computation.8 | async-start | bytes 1179648 | tf_op jit(solution)/shard_map/psum | solution.py:189
  438.0 9.1 %copy-start.4 = (bf16[8,12,6,6,256]{4,3,2,1,0:T(8,128)(2,1)S(1)}, bf16[8,12,6,6,256]{4,3,2,1,0:T(8,128)(2,1)}, u32[]{:S(2)}) copy-start(bf16[8,12,6,6,256]{4,3,2,1,0:T(8,128)(2,1)} %fusion.39) | copy-start | bytes 5308420
  450.4 49.5 %copy-start.10 = (f32[576,256]{1,0:T(8,128)S(1)}, f32[576,256]{1,0:T(8,128)}, u32[]{:S(2)}) copy-start(f32[576,256]{1,0:T(8,128)} %param.33) | copy-start | bytes 1769476
  450.4 49.5 %copy-start.20 = (f32[576,256]{1,0:T(8,128)S(1)}, f32[576,256]{1,0:T(8,128)}, u32[]{:S(2)}) copy-start(f32[576,256]{1,0:T(8,128)} %param.36) | copy-start | bytes 1769476
  450.4 49.5 %copy-start.21 = (f32[576,256]{1,0:T(8,128)S(1)}, f32[576,256]{1,0:T(8,128)}, u32[]{:S(2)}) copy-start(f32[576,256]{1,0:T(8,128)} %param.37) | copy-start | bytes 1769476
  450.4 51.9 %copy-start.12 = (f32[576,256]{1,0:T(8,128)S(1)}, f32[576,256]{1,0:T(8,128)}, u32[]{:S(2)}) copy-start(f32[576,256]{1,0:T(8,128)} %param.34) | copy-start | bytes 1769476
  450.4 51.9 %copy-start.22 = (f32[576,256]{1,0:T(8,128)S(1)}, f32[576,256]{1,0:T(8,128)}, u32[]{:S(2)}) copy-start(f32[576,256]{1,0:T(8,128)} %param.38) | copy-start | bytes 1769476
  450.4 51.9 %copy-start.23 = (f32[576,256]{1,0:T(8,128)S(1)}, f32[576,256]{1,0:T(8,128)}, u32[]{:S(2)}) copy-start(f32[576,256]{1,0:T(8,128)} %param.39) | copy-start | bytes 1769476
Sparse Core Ops, SparseCore 0:
  13.8 21.8 reduce-scatter.9
  38.0 30.0 all-gather.2
  70.2 29.5 all-gather.4
  281.0 26.5 reduce-scatter.7
  412.5 26.7 reduce-scatter.5
  447.2 52.5 all-reduce.42
where the time goes:
time: 519 us; the launch traced here: 512 us
  local copies, waits for them, and re-layouts  163 us (31%)
  matrix products  139 us (27%)
  other arithmetic  98.3 us (19%)
  waiting for transfers between devices  56.7 us (11%)
  blocking collectives  38.4 us (7%)
  between operations  15.6 us (3%)
    squeeze x2, local copies, waits for them, and re-layouts, conv_back(): moved = jnp.pad(pulled[:, :, :, :, tap_index], widths)  62.2 us
    unnamed x82, local copies, waits for them, and re-layouts  49.7 us
    dot_general x2, matrix products, conv_apply(): jnp.einsum('pc,tcd->ptd', flat_padded, taps_weight, preferred_element_typ...  46.2 us
    psum x1, waiting for transfers between devices, per_device(): lax.psum(shards[0].astype(jnp.bfloat16), 'dp').astype(jnp.float32)  45.6 us
    dot_general x2, matrix products, conv_back(): jnp.einsum('pd,tcd->ptc', flat_grad, taps_weight, preferred_element_type=...  36.3 us
    add x2, other arithmetic, conv_back(): spread = moved if spread is None else spread + moved  33.3 us
    dot_general x2, matrix products, conv_back(): jnp.einsum('pc,ptd->tcd', flat_padded, stacked, preferred_element_type=jn...  29.2 us
    psum x1, blocking collectives, per_device(): lax.psum(shards[2].astype(jnp.bfloat16), 'dp').astype(jnp.float32)  23.7 us
  transfers between devices with their start and end apart: 6, of which 2 were waited for; matrix products, arithmetic and copies ran while one was open for 45% of the time, Pallas kernels for 0%

commit v1 on v0

--- a/solution.py
+++ b/solution.py
@@ -6,6 +6,27 @@
 C = 256
 STEP_COUNT = 10
 tap_offsets = [(row_off, col_off) for row_off in range(3) for col_off in range(3)]
+
+
+def collect(x, axis, dim):
+    length, here, width = (lax.axis_size(axis), lax.axis_index(axis), x.shape[dim])
+    forward = [(i, (i + 1) % length) for i in range(length)]
+    downward = [(i, (i - 1) % length) for i in range(length)]
+    whole = jnp.zeros((*x.shape[:dim], length * width, *x.shape[dim + 1 :]), x.dtype)
+    whole = lax.dynamic_update_slice_in_dim(whole, x, here * width, axis=dim)
+    from_left = from_right = x
+    half = length // 2
+    for hop in range(1, half + 1):
+        from_left = lax.ppermute(from_left, axis, forward)
+        whole = lax.dynamic_update_slice_in_dim(
+            whole, from_left, (here - hop) % length * width, axis=dim
+        )
+        if hop < length - half:
+            from_right = lax.ppermute(from_right, axis, downward)
+            whole = lax.dynamic_update_slice_in_dim(
+                whole, from_right, (here + hop) % length * width, axis=dim
+            )
+    return whole
 
 
 def face_hots(face_table, dtype):
@@ -140,7 +161,7 @@
     gathered = (
         lax.all_gather(low_weights[0], "fsdp", axis=0, tiled=True),
         lax.all_gather(low_weights[1], "fsdp", axis=0, tiled=True),
-        lax.all_gather(low_weights[2], "fsdp", axis=0, tiled=True),
+        collect(low_weights[2], "fsdp", 0),
     )
     saved = forward_pass(fields, hots_low, gathered)
     flat_fields = fields.reshape(-1, channels)

time: 519 us -> 544 us (1.048)
  local copies, waits for them, and re-layouts: 163 us -> 182 us
  other arithmetic: 98.3 us -> 105 us
    reduce_scatter x1, waiting for transfers between devices: 11 us -> 0.01 us  [per_device(): lax.psum_scatter(dw_skip.astype(jnp.bfloat16), 'fsdp', scatter_dimension=...]
    ppermute x0 -> x3, starting transfers between devices: none -> 5.82 us  [the longest x1 5.05 us: collect(): from_right = lax.ppermute(from_right, axis, downward)]
    unnamed x82 -> x91, local copies, waits for them, and re-layouts: 49.7 us -> 52 us
  transfers between devices with their start and end apart: 6 -> 9, of which waited for: 2 -> 2; matrix products, arithmetic and copies ran while one was open for 45% -> 47% of each run, Pallas kernels for 0% -> 0%
where the time goes in v1:
time: 544 us; the launch traced here: 535 us
  local copies, waits for them, and re-layouts  182 us (33%)
  matrix products  135 us (25%)
  other arithmetic  105 us (19%)
  waiting for transfers between devices  51.4 us (9%)
  blocking collectives  40.5 us (7%)
  between operations  15.6 us (3%)
  starting transfers between devices  6.07 us (1%)
    squeeze x2, local copies, waits for them, and re-layouts, conv_back(): moved = jnp.pad(pulled[:, :, :, :, tap_index], widths)  62.2 us
    unnamed x91, local copies, waits for them, and re-layouts  52 us
    psum x1, waiting for transfers between devices, per_device(): lax.psum(shards[0].astype(jnp.bfloat16), 'dp').astype(jnp.float32)  47 us
    dot_general x2, matrix products, conv_apply(): jnp.einsum('pc,tcd->ptd', flat_padded, taps_weight, preferred_element_typ...  45.8 us
    dot_general x2, matrix products, conv_back(): jnp.einsum('pd,tcd->ptc', flat_grad, taps_weight, preferred_element_type=...  36.3 us
    add x2, other arithmetic, conv_back(): spread = moved if spread is None else spread + moved  33.5 us
    dot_general x2, matrix products, conv_back(): jnp.einsum('pc,ptd->tcd', flat_padded, stacked, preferred_element_type=jn...  29.2 us
    psum x1, blocking collectives, per_device(): lax.psum(shards[2].astype(jnp.bfloat16), 'dp').astype(jnp.float32)  23.9 us
  transfers between devices with their start and end apart: 9, of which 2 were waited for; matrix products, arithmetic and copies ran while one was open for 47% of the time, Pallas kernels for 0%

profile of v1, /device:TPU:0, one launch (start us, length us, event | category | flops | bytes accessed | tf_op | source)
XLA Modules:
  0.0 535.4 jit_solution(11358094174102996031)
XLA Ops:
  7.9 5.0 fusion.79
  16.0 5.0 collective-permute-start.1
  21.0 1.8 convert_element_type.235
  22.9 1.9 copy.310
  24.8 2.4 copy.501
  27.3 2.2 fusion.35
  29.4 4.1 reshape_squeeze.3
  38.5 2.4 maximum_bitcast_fusion
  41.0 16.6 %all_gather.13 = bf16[256,256]{1,0:T(8,128)(2,1)} all-gather(bf16[64,256]{1,0:T(8,128)(2,1)} %get-tuple-element.167), channel_id=1, replica_groups=mesh['dp'=8,'fsdp'=4] {'fsdp'}, dimensions={0}, use_global_device_ids=true | all-gather | bytes 163840 | tf_op jit(solution)/shard_map/all_gather | solution.py:175
  59.9 4.3 collective-permute-done.2
  64.9 2.9 copy.311
  67.8 4.9 reshape.701
  72.7 23.9 %psum.23 = bf16[64,256]{1,0:T(8,128)(2,1)S(1)} all-reduce(bf16[64,256]{1,0:T(8,128)(2,1)} %reduce-scatter.10.cloned.1.call-done), channel_id=1, replica_groups=mesh['dp'=8,'fsdp'=4] {'dp'}, use_global_device_ids=true, to_apply=%region_5.6 | all-reduce | flops 16384 | bytes 65536 | tf_op jit(solution)/shard_map/psum | solution.py:212
  97.3 23.2 %fusion.33 = f32[8,12,8,8,9,256]{5,3,4,2,1,0:T(8,128)} fusion(bf16[9,256,256,1,1,1]{2,1,0,5,4,3:T(8,128)(2,1)} %bitcast.402, bf16[8,12,8,8,256,1]{4,1,3,0,2,5:T(8,128)(2,1)} %maximum_bitcast_fusion), kind=kOutput, calls=%fused_computation.103 | convolution fusion | flops 7247757312 | bytes 60948480 | tf_op jit(solution)/shard_map/pc,tcd->ptd/dot_general | solution.py:81
  120.5 17.8 %multiply_convert_fusion = (bf16[8,12,6,6,256]{4,3,2,1,0:T(8,128)(2,1)S(1)}, f32[8,12,6,6,256]{4,3,2,1,0:T(8,128)}) fusion(f32[8,12,8,8,9,256]{5,3,4,2,1,0:T(8,128)} %fusion.33), kind=kLoop, calls=%fused_computation.79 | loop fusion | flops 15040512 | bytes 37158912 | tf_op jit(solution)/shard_map/convert_element_type | solution.py:120
  144.6 22.6 %fusion.110 = f32[8,12,8,8,9,256]{5,3,2,1,0,4:T(8,128)} fusion(bf16[9,256,256,1,1,1]{2,1,5,4,3,0:T(8,128)(2,1)} %bitcast.400, bf16[8,12,1,8,256]{4,3,2,1,0:T(8,128)(2,1)} %copy.300, bf16[8,12,6,1,256]{4,3,2,1,0:T(2,128)(2,1)S(1)} %copy.295, bf16[8,12,6,6,256]{4,3,2,1,0:T(8,128)(2,1)S(1)} %get-tuple-element.164, bf16[8,12,6,1,256]{4,3,2,1,0:T(2,128)(2,1)S(1)} %copy.294, ...), kind=kOutput, calls=%fused_computation.208 | convolution fusion | flops 7263485952 | bytes 60948480 | tf_op jit(solution)/shard_map/pc,tcd->ptd/dot_general | solution.py:81
  167.2 18.1 %fusion.7 = (bf16[8,12,6,6,256]{4,3,2,1,0:T(8,128)(2,1)S(1)}, f32[8,12,6,6,1,256]{5,3,2,1,0,4:T(8,128)}) fusion(bf16[8]{0:T(256)(128)(2,1)S(1)} %copy-done.33, bf16[1,8,12,6,6,256]{5,1,4,3,2,0:T(8,128)(2,1)S(1)} %copy-done.1, f32[8,12,8,8,9,256]{5,3,2,1,0,4:T(8,128)} %fusion.110), kind=kLoop, calls=%fused_computation.20 | loop fusion | flops 26542080 | bytes 38928400 | tf_op jit(solution)/shard_map/convert_element_type | solution.py:186
  185.3 19.7 %fusion.36 = f32[8,12,6,6,9,256]{5,3,2,1,0,4:T(8,128)} fusion(bf16[9,256,256,1,1,1]{2,1,5,4,3,0:T(8,128)(2,1)S(1)} %bitcast.401, f32[8,12,6,6,1,256]{5,3,2,1,0,4:T(8,128)} %get-tuple-element.163, bf16[1,8,12,6,6,256]{5,1,4,3,2,0:T(8,128)(2,1)} %param.30, bf16[8]{0:T(256)(128)(2,1)} %copy-done.32), kind=kOutput, calls=%fused_computation.110 | convolution fusion | flops 4098097152 | bytes 38338576 | tf_op jit(solution)/shard_map/pd,tcd->ptc/dot_general | solution.py:96
  205.0 30.6 %slice_bitcast_fusion.17 = (f32[8,12,6,6,256]{4,3,2,1,0:T(8,128)}, f32[8,12,6,6,256]{4,3,2,1,0:T(8,128)}, f32[8,12,6,6,256]{4,3,2,1,0:T(8,128)}, f32[8,12,6,6,25...) fusion(f32[8,12,6,6,9,256]{5,3,2,1,0,4:T(8,128)} %fusion.36), kind=kLoop, calls=%fused_computation.57 | loop fusion | bytes 63700992 | tf_op jit(solution)/shard_map/squeeze | solution.py:102
  235.6 18.5 %pad_add_fusion.1 = f32[8,12,8,8,256]{4,3,2,1,0:T(8,128)} fusion(f32[8,12,6,6,256]{4,3,2,1,0:T(8,128)} %get-tuple-element.185, f32[8,12,6,6,256]{4,3,2,1,0:T(8,128)} %get-tuple-element.178, f32[8,12,6,6,256]{4,3,2,1,0:T(8,128)} %get-tuple-element.179, f32[8,12,6,6,256]{4,3,2,1,0:T(8,128)} %get-tuple-element.180, f32[8,12,6,6,256]{4,3,2,1,0:T(8,128)} %get-tuple-element.181, ...), kind=kLoop, calls=%fused_computation.7 | loop fusion | flops 12582912 | bytes 38141952 | tf_op jit(solution)/shard_map/add | solution.py:103
  254.1 4.9 fusion.169
  259.0 2.7 slice_bitcast_fusion.26
  261.7 5.3 slice.563
  267.0 2.3 bitcast_dynamic-update-slice_fusion.8
  269.3 2.5 bitcast_dynamic-update-slice_fusion.7
  271.7 2.5 bitcast_dynamic-update-slice_fusion.6
  274.2 2.4 bitcast_dynamic-update-slice_fusion.5
  276.6 2.4 bitcast_dynamic-update-slice_fusion.4
  279.0 2.4 bitcast_dynamic-update-slice_fusion.3
  281.5 2.4 bitcast_dynamic-update-slice_fusion.2
  283.9 2.5 bitcast_dynamic-update-slice_fusion.1
  286.3 2.4 bitcast_dynamic-update-slice_fusion
  288.7 13.9 %bitcast_convert_fusion = bf16[9,256,256]{1,2,0:T(8,128)(2,1)} fusion(bf16[8,12,8,8,9,256]{5,3,2,1,0,4:T(8,128)(2,1)} %bitcast_dynamic-update-slice_fusion, bf16[8,12,1,8,256]{4,3,2,1,0:T(8,128)(2,1)S(1)} %copy-done.20, bf16[8,12,6,1,256]{4,3,2,1,0:T(2,128)(2,1)S(1)} %copy-done.18, bf16[8,12,6,6,256]{4,3,2,1,0:T(8,128)(2,1)S(1)} %copy-done.3, ...), kind=kOutput, calls=%fused_computation.108 | convolution fusion | flops 7264075776 | bytes 32636928 | tf_op jit(solution)/shard_map/pc,ptd->tcd/dot_general | solution.py:107
  305.2 2.5 fusion.85
  307.7 3.2 slice_add_fusion.19
  310.9 13.4 %scatter-add.29 = f32[8,12,6,6,256]{4,3,2,1,0:T(8,128)} dynamic-update-slice(f32[8,12,6,6,256]{4,3,2,1,0:T(8,128)} %fusion.85, f32[8,12,6,1,256]{4,3,2,1,0:T(1,128)S(1)} %slice_add_fusion.19, s32[]{:T(128)} %constant.253.clone.1, s32[]{:T(128)} %constant.253.clone.1, s32[]{:T(128)} %constant.253.clone.1, s32[]{:T(128)} %constant.253.clone.1, s32[]{:T(128)} %constant.253.clone.1) | dynamic-update-slice | bytes 1179652 | tf_op jit(solution)/shard_map/scatter-add | solution.py:64
  324.3 2.5 fusion.84
  326.8 3.4 slice_add_fusion.18
  330.2 12.9 %scatter-add.31 = f32[8,12,6,6,256]{4,3,2,1,0:T(8,128)} dynamic-update-slice(f32[8,12,6,6,256]{4,3,2,1,0:T(8,128)} %fusion.84, f32[8,12,6,1,256]{4,3,2,1,0:T(1,128)S(1)} %slice_add_fusion.18, s32[]{:T(128)} %constant.253.clone.1, s32[]{:T(128)} %constant.253.clone.1, s32[]{:T(128)} %constant.253.clone.1, s32[]{:T(128)} %constant.263.clone.1, s32[]{:T(128)} %constant.253.clone.1) | dynamic-update-slice | bytes 1179652 | tf_op jit(solution)/shard_map/scatter-add | solution.py:70
  343.1 5.5 %fusion.16 = bf16[8,12,6,6,256]{4,3,2,1,0:T(8,128)(2,1)S(1)} fusion(f32[8,12,6,6,256]{4,3,2,1,0:T(8,128)} %get-tuple-element.165, f32[8,12,6,6,256]{4,3,2,1,0:T(8,128)} %scatter-add.31), kind=kLoop, calls=%fused_computation.29 | loop fusion | flops 17694720 | bytes 8847360 | tf_op jit(solution)/shard_map/convert_element_type | solution.py:190
  348.7 2.3 bitcast_dynamic-update-slice_fusion.17
  350.9 2.4 bitcast_dynamic-update-slice_fusion.16
  353.4 2.4 bitcast_dynamic-update-slice_fusion.15
  355.8 2.3 bitcast_dynamic-update-slice_fusion.14
  358.1 2.5 bitcast_dynamic-update-slice_fusion.13
  360.5 2.4 bitcast_dynamic-update-slice_fusion.12
  363.0 2.3 bitcast_dynamic-update-slice_fusion.11
  365.3 2.4 bitcast_dynamic-update-slice_fusion.10
  367.8 2.5 bitcast_dynamic-update-slice_fusion.9
  370.2 16.7 %fusion.41 = f32[8,12,6,6,9,256]{5,1,4,3,2,0:T(8,128)} fusion(bf16[9,256,256,1,1,1]{2,1,0,5,4,3:T(8,128)(2,1)S(1)} %bitcast.403, bf16[8,12,6,6,256,1]{4,3,2,1,0,5:T(8,128)(2,1)S(1)} %bitcast.394), kind=kOutput, calls=%fused_computation.115 | convolution fusion | flops 4076863488 | bytes 34799616 | tf_op jit(solution)/shard_map/pd,tcd->ptc/dot_general | solution.py:96
  386.9 31.6 %slice_bitcast_fusion.8 = (f32[8,12,6,6,256]{4,1,3,2,0:T(8,128)}, f32[8,12,6,6,256]{4,1,3,2,0:T(8,128)}, f32[8,12,6,6,256]{4,1,3,2,0:T(8,128)}, f32[8,12,6,6,256...) fusion(f32[8,12,6,6,9,256]{5,1,4,3,2,0:T(8,128)} %fusion.41), kind=kLoop, calls=%fused_computation.48 | loop fusion | bytes 63700992 | tf_op jit(solution)/shard_map/squeeze | solution.py:102
  418.5 15.3 %bitcast_convert_fusion.1 = bf16[9,256,256]{1,2,0:T(8,128)(2,1)} fusion(bf16[8,12,8,8,9,256]{5,3,2,1,0,4:T(8,128)(2,1)} %bitcast_dynamic-update-slice_fusion.9, bf16[8,12,8,8,256,1]{4,1,3,0,2,5:T(8,128)(2,1)} %maximum_bitcast_fusion), kind=kOutput, calls=%fused_computation.109 | convolution fusion | flops 7248347136 | bytes 32636928 | tf_op jit(solution)/shard_map/pc,ptd->tcd/dot_general | solution.py:107
  433.9 5.4 %fusion.29 = bf16[1,8,12,6,6,256]{5,4,3,2,1,0:T(8,128)(2,1)S(1)} fusion(f32[1,8,12,6,6,256]{5,4,3,2,1,0:T(8,128)} %reshape.701, f32[8,12,6,6,1,256]{5,3,2,1,0,4:T(8,128)} %get-tuple-element.163), kind=kLoop, calls=%fused_computation.77 | loop fusion | flops 8847360 | bytes 8847360 | tf_op jit(solution)/shard_map/convert_element_type | solution.py:171
  439.3 3.1 copy.351
  442.4 15.0 %pad_add_fusion = f32[8,12,8,8,256]{4,1,3,2,0:T(8,128)S(1)} fusion(f32[8,12,6,6,256]{4,1,3,2,0:T(8,128)} %get-tuple-element.175, f32[8,12,6,6,256]{4,1,3,2,0:T(8,128)} %get-tuple-element.176, f32[8,12,6,6,256]{4,1,3,2,0:T(8,128)} %get-tuple-element.169, f32[8,12,6,6,256]{4,1,3,2,0:T(8,128)} %get-tuple-element.170, f32[8,12,6,6,256]{4,1,3,2,0:T(8,128)} %get-tuple-element.171, ...), kind=kLoop, calls=%fused_computation | loop fusion | flops 12582912 | bytes 38141952 | tf_op jit(solution)/shard_map/add | solution.py:103
  457.4 2.7 slice.581
  461.6 2.5 fusion.58
  464.1 2.6 fusion.60
  466.7 2.6 fusion.62
  469.3 3.3 add_bitcast_fusion
  472.6 3.8 copy.352
  476.5 47.0 %all-reduce.43.cloned.1.call-done = (bf16[576,256]{1,0:T(8,128)(2,1)}, bf16[576,256]{1,0:T(8,128)(2,1)}) async-done(((bf16[576,256]{1,0:T(8,128)(2,1)}, bf16[576,256]{1,0:T(8,128)(2,1)}), (bf16[576,256]{1,0:T(8,128)(2,1)}, bf16[576,256]{1,0:T(8,128)(2,1)})) %all-reduce.43.cloned.1.call-update) | async-done | bytes 589840 | tf_op jit(solution)/shard_map/psum | solution.py:210
  523.5 2.4 multiply_subtract_fusion.1
  525.9 2.4 multiply_subtract_fusion
  (131 shorter events, 21.9 us)
Async XLA Ops:
  7.2 65.5 %reduce-scatter.10.cloned.1.call-start = ((), (), s32[]{:S(2)}) async-start(), calls=%async_computation.7 | async-start | bytes 163840 | tf_op jit(solution)/shard_map/reduce_scatter | solution.py:203
  7.9 19.4 %copy-start.32 = (bf16[8]{0:T(256)(128)(2,1)}, bf16[8]{0:T(256)(128)(2,1)S(1)}, u32[]{:S(2)}) copy-start(bf16[8]{0:T(256)(128)(2,1)S(1)} %compare_convert_fusion) | copy-start | bytes 52
  7.9 5.9 %copy-start.12 = (f32[576,256]{1,0:T(8,128)S(1)}, f32[576,256]{1,0:T(8,128)}, u32[]{:S(2)}) copy-start(f32[576,256]{1,0:T(8,128)} %param.33) | copy-start | bytes 1769476
  7.9 6.8 %copy-start.28 = (f32[64,256]{1,0:T(8,128)S(1)}, f32[64,256]{1,0:T(8,128)}, u32[]{:S(2)}) copy-start(f32[64,256]{1,0:T(8,128)} %param.35) | copy-start | bytes 196612
  7.9 15.0 %copy-start.6 = (bf16[1,8,12,6,6,256]{5,1,4,3,2,0:T(8,128)(2,1)S(1)}, bf16[1,8,12,6,6,256]{5,1,4,3,2,0:T(8,128)(2,1)}, u32[]{:S(2)}) copy-start(bf16[1,8,12,6,6,256]{5,1,4,3,2,0:T(8,128)(2,1)} %param.29) | copy-start | bytes 5308420
  13.8 83.5 %all-gather.3.cloned.1.call-start = ((), (), s32[]{:S(2)}) async-start(), calls=%async_computation.3 | async-start | bytes 1474560 | tf_op jit(solution)/shard_map/all_gather | solution.py:162
  14.6 129.2 %all-gather.5.cloned.1.call-start = ((), (), s32[]{:S(2)}) async-start(), calls=%async_computation.4 | async-start | bytes 1474560 | tf_op jit(solution)/shard_map/all_gather | solution.py:163
  15.3 0.7 copy-start.26
  15.9 11.3 %copy-start = (bf16[1,8,12,6,6,256]{5,1,4,3,2,0:T(8,128)(2,1)S(1)}, bf16[1,8,12,6,6,256]{5,1,4,3,2,0:T(8,128)(2,1)}, u32[]{:S(2)}) copy-start(bf16[1,8,12,6,6,256]{5,1,4,3,2,0:T(8,128)(2,1)} %param.30) | copy-start | bytes 5308420
  16.0 43.2 %collective-permute-start.1 = (bf16[64,256]{1,0:T(8,128)(2,1)}, bf16[64,256]{1,0:T(8,128)(2,1)}, u32[]{:S(2)}, u32[]{:S(2)}) collective-permute-start(bf16[64,256]{1,0:T(8,128)(2,1)} %get-tuple-element.167), channel_id=1, source_target_pairs={{0,3},{1,0},{2,1},{3,2},{4,7},{5,4},{6,5},{7,6},{8,11},{9,8},{10,9... | collective-permute-start | bytes 98312 | tf_op jit(solution)/shard_map/ppermute | solution.py:25
  21.0 36.6 %collective-permute-start = (bf16[64,256]{1,0:T(8,128)(2,1)}, bf16[64,256]{1,0:T(8,128)(2,1)}, u32[]{:S(2)}, u32[]{:S(2)}) collective-permute-start(bf16[64,256]{1,0:T(8,128)(2,1)} %get-tuple-element.167), channel_id=1, source_target_pairs={{0,1},{1,2},{2,3},{3,0},{4,5},{5,6},{6,7},{7,4},{8,9},{9,10},{10,1... | collective-permute-start | bytes 98312 | tf_op jit(solution)/shard_map/ppermute | solution.py:20
  22.8 446.4 %reduce-scatter.8.cloned.1.call-start = ((), (), s32[]{:S(2)}) async-start(), calls=%async_computation.6 | async-start | bytes 1474560 | tf_op jit(solution)/shard_map/reduce_scatter | solution.py:200
  24.8 4.6 copy-start.34
  29.4 5.4 copy-start.4
  38.5 19.8 %copy-start.27 = (bf16[256,256]{1,0:T(8,128)(2,1)S(1)}, bf16[256,256]{1,0:T(8,128)(2,1)}, u32[]{:S(2)}) copy-start(bf16[256,256]{1,0:T(8,128)(2,1)} %copy-done.26) | copy-start | bytes 393220
  38.5 25.6 %copy-start.7 = (bf16[3456,256]{1,0:T(8,128)(2,1)S(1)}, bf16[3456,256]{1,0:T(8,128)(2,1)}, u32[]{:S(2)}) copy-start(bf16[3456,256]{1,0:T(8,128)(2,1)} %reshape_squeeze.3) | copy-start | bytes 5308420
  57.6 6.6 %collective-permute-start.2 = (bf16[64,256]{1,0:T(8,128)(2,1)}, bf16[64,256]{1,0:T(8,128)(2,1)S(1)}, u32[]{:S(2)}, u32[]{:S(2)}) collective-permute-start(bf16[64,256]{1,0:T(8,128)(2,1)} %collective-permute-done), channel_id=1, source_target_pairs={{0,1},{1,2},{2,3},{3,0},{4,5},{5,6},{6,7},{7,4},{8,9},{9,10},{10,1... | collective-permute-start | bytes 98312 | tf_op jit(solution)/shard_map/ppermute | solution.py:20
  67.8 28.8 %copy-start.29 = (f32[64,256]{1,0:T(8,128)S(1)}, f32[64,256]{1,0:T(8,128)}, u32[]{:S(2)}) copy-start(f32[64,256]{1,0:T(8,128)} %param.35) | copy-start | bytes 196612
  67.8 28.8 %copy-start.30 = (f32[64,256]{1,0:T(8,128)S(1)}, f32[64,256]{1,0:T(8,128)}, u32[]{:S(2)}) copy-start(f32[64,256]{1,0:T(8,128)} %param.40) | copy-start | bytes 196612
  67.8 28.8 %copy-start.31 = (f32[64,256]{1,0:T(8,128)S(1)}, f32[64,256]{1,0:T(8,128)}, u32[]{:S(2)}) copy-start(f32[64,256]{1,0:T(8,128)} %param.41) | copy-start | bytes 196612
  138.3 5.5 %copy-start.2 = (bf16[8,12,6,6,256]{4,3,2,1,0:T(8,128)(2,1)}, bf16[8,12,6,6,256]{4,3,2,1,0:T(8,128)(2,1)S(1)}, u32[]{:S(2)}) copy-start(bf16[8,12,6,6,256]{4,3,2,1,0:T(8,128)(2,1)S(1)} %get-tuple-element.164) | copy-start | bytes 5308420
  143.0 0.9 copy-start.15
  143.8 0.8 copy-start.17
  144.6 22.7 %copy-start.1 = (bf16[1,8,12,6,6,256]{5,1,4,3,2,0:T(8,128)(2,1)S(1)}, bf16[1,8,12,6,6,256]{5,1,4,3,2,0:T(8,128)(2,1)}, u32[]{:S(2)}) copy-start(bf16[1,8,12,6,6,256]{5,1,4,3,2,0:T(8,128)(2,1)} %param.30) | copy-start | bytes 5308420
  144.6 22.7 %copy-start.33 = (bf16[8]{0:T(256)(128)(2,1)S(1)}, bf16[8]{0:T(256)(128)(2,1)}, u32[]{:S(2)}) copy-start(bf16[8]{0:T(256)(128)(2,1)} %copy-done.32) | copy-start | bytes 52
  167.2 18.1 %copy-start.8 = (bf16[2304,256]{1,0:T(8,128)(2,1)S(1)}, bf16[2304,256]{1,0:T(8,128)(2,1)}, u32[]{:S(2)}) copy-start(bf16[2304,256]{1,0:T(8,128)(2,1)} %all-gather.5.cloned.1.call-done) | copy-start | bytes 3538948
  283.8 4.9 copy-start.3
  283.8 4.9 copy-start.16
  283.8 4.9 copy-start.18
  283.8 4.9 copy-start.19
  283.8 4.9 copy-start.20
  302.6 1.1 copy-start.11
  302.6 1.8 copy-start.10
  302.7 166.6 %reduce-scatter.6.cloned.1.call-start = ((), (), s32[]{:S(2)}) async-start(), calls=%async_computation.5 | async-start | bytes 1474560 | tf_op jit(solution)/shard_map/reduce_scatter | solution.py:197
  365.3 4.9 copy-start.9
  433.8 89.6 %all-reduce.43.cloned.1.call-start = ((), (), s32[]{:S(2)}) async-start(), calls=%async_computation.8 | async-start | bytes 1179648 | tf_op jit(solution)/shard_map/psum | solution.py:210
  460.1 9.1 %copy-start.5 = (bf16[8,12,6,6,256]{4,3,2,1,0:T(8,128)(2,1)S(1)}, bf16[8,12,6,6,256]{4,3,2,1,0:T(8,128)(2,1)}, u32[]{:S(2)}) copy-start(bf16[8,12,6,6,256]{4,3,2,1,0:T(8,128)(2,1)} %fusion.35) | copy-start | bytes 5308420
  460.2 9.1 %copy-start.25 = (bf16[256,256]{1,0:T(8,128)(2,1)S(1)}, bf16[256,256]{1,0:T(8,128)(2,1)}, u32[]{:S(2)}) copy-start(bf16[256,256]{1,0:T(8,128)(2,1)} %all_gather.13) | copy-start | bytes 393220
  472.6 50.9 %copy-start.13 = (f32[576,256]{1,0:T(8,128)S(1)}, f32[576,256]{1,0:T(8,128)}, u32[]{:S(2)}) copy-start(f32[576,256]{1,0:T(8,128)} %param.33) | copy-start | bytes 1769476
  472.6 50.9 %copy-start.21 = (f32[576,256]{1,0:T(8,128)S(1)}, f32[576,256]{1,0:T(8,128)}, u32[]{:S(2)}) copy-start(f32[576,256]{1,0:T(8,128)} %param.36) | copy-start | bytes 1769476
  472.6 50.9 %copy-start.22 = (f32[576,256]{1,0:T(8,128)S(1)}, f32[576,256]{1,0:T(8,128)}, u32[]{:S(2)}) copy-start(f32[576,256]{1,0:T(8,128)} %param.37) | copy-start | bytes 1769476
  472.6 53.3 %copy-start.14 = (f32[576,256]{1,0:T(8,128)S(1)}, f32[576,256]{1,0:T(8,128)}, u32[]{:S(2)}) copy-start(f32[576,256]{1,0:T(8,128)} %param.34) | copy-start | bytes 1769476
  472.6 53.3 %copy-start.23 = (f32[576,256]{1,0:T(8,128)S(1)}, f32[576,256]{1,0:T(8,128)}, u32[]{:S(2)}) copy-start(f32[576,256]{1,0:T(8,128)} %param.38) | copy-start | bytes 1769476
  472.6 53.3 %copy-start.24 = (f32[576,256]{1,0:T(8,128)S(1)}, f32[576,256]{1,0:T(8,128)}, u32[]{:S(2)}) copy-start(f32[576,256]{1,0:T(8,128)} %param.39) | copy-start | bytes 1769476
Sparse Core Ops, SparseCore 0:
  13.9 21.8 reduce-scatter.9
  38.0 30.5 all-gather.2
  70.8 30.1 all-gather.4
  302.8 27.9 reduce-scatter.7
  434.0 28.1 reduce-scatter.5
  469.4 54.0 all-reduce.42
